TPU v7x, 32 devices: a whole 2x2x4 slice. The times are simulated.
32 devices in a mesh: row: 8 (over y, x, core), col: 4 (over z).
Axes of the slice: x: 2, y: 2, z: 4, core: 2. Of those that a mesh axis runs over, the one named last changes fastest.
Arguments:
- object_field: float32 [2, 4096, 2048], P(None, 'row', 'col'), may hold values from -6 to 6
- probe: float32 [3, 2, 256, 256], replicated, may hold values from -6 to 6
- raw_counts: bfloat16 [192, 256, 256], P(('row', 'col')), may hold values from 0.099609375 to 10
- resample_delta: float32 [256, 256], replicated, may hold values from -0.1875 to 0.1875
- tile_row: int32 [192, 1], P(('row', 'col')), may hold values from 0 to 7; in each aligned block of 6 rows (0 to 5, 6 to 11, ...) no two rows name the same one
- offsets: int32 [192, 2], P(('row', 'col')), may hold values from 0 to 511
Outputs:
- object_grad: float32 [2, 4096, 2048], P(None, 'row', 'col')
- probe_grad: float32 [3, 2, 256, 256], replicated
Inputs may be any that keep to these rules, and one draw needn't show every extreme that they name: `tile_row`: the 6 frames of one device have distinct tile rows.
All inputs are finite; a program needn't handle non-finite values.
Results may differ from a plain program's by a relative error of at most 0.0008.
The roundings to bfloat16 on the way count: a program that leaves them out, or rounds other values in their place, can miss the bound.
Values may be sent and summed in bfloat16 or wider, within the bound.
A program may use at most 128 MiB of HBM per device.

v0:
```python
import math

import jax
import jax.numpy as jnp
from jax import lax
from jax.sharding import PartitionSpec as P


def extended_2(value, sides, width):
    for axis, dim in sides:
        size, length = (lax.axis_size(axis), value.shape[dim])
        up = [(i, (i + 1) % size) for i in range(size - 1)]
        down = [(j, i) for i, j in up]
        last = lax.slice_in_dim(value, length - width, length, axis=dim)
        first = lax.slice_in_dim(value, 0, width, axis=dim)
        before = lax.ppermute(last, axis, up)
        after = lax.ppermute(first, axis, down)
        value = jnp.concatenate([before, value, after], axis=dim)
    return value


def product(left, right):
    return jnp.dot(left, right, preferred_element_type=jnp.float32)


def dft_tables(points):
    indices = jnp.arange(points, dtype=jnp.int32)
    phases = indices[:, None] * indices[None, :] % points
    angles = phases.astype(jnp.float32) * (2.0 * math.pi / points)
    norming = 1.0 / math.sqrt(points)
    cosine = jnp.cos(angles) * norming
    sine_part = -jnp.sin(angles) * norming
    forward = jnp.concatenate(
        [jnp.concatenate([cosine, -sine_part], 1), jnp.concatenate([sine_part, cosine], 1)], 0
    )
    backward = jnp.concatenate(
        [jnp.concatenate([cosine, sine_part], 1), jnp.concatenate([-sine_part, cosine], 1)], 0
    )
    return (forward.astype(jnp.bfloat16), backward.astype(jnp.bfloat16))


def measure(raw_counts, resample_delta):
    points = resample_delta.shape[0]
    resample = (jnp.eye(points, dtype=jnp.float32) + resample_delta).astype(jnp.bfloat16)
    first = jnp.einsum(
        "ij,kjl->kil", resample, raw_counts, preferred_element_type=jnp.float32
    ).astype(jnp.bfloat16)
    second = jnp.einsum("kij,lj->kil", first, resample, preferred_element_type=jnp.float32)
    return jnp.sqrt(jnp.maximum(second, 0.0)).astype(jnp.bfloat16)


def frame_terms(window, probe, amplitude, forward, backward):
    mode_count = probe.shape[0]
    points = probe.shape[-1]
    probe_real = probe[:, 0]
    probe_imag = probe[:, 1]
    object_real = window[0]
    object_imag = window[1]
    wave = jnp.stack(
        [
            probe_real * object_real - probe_imag * object_imag,
            probe_real * object_imag + probe_imag * object_real,
        ],
        1,
    )
    wave_cols = (
        wave.transpose(1, 2, 0, 3).reshape(2 * points, mode_count * points).astype(jnp.bfloat16)
    )
    half_done = product(forward, wave_cols).astype(jnp.bfloat16)
    wave_rows = (
        half_done.reshape(2, points, mode_count, points)
        .transpose(2, 1, 0, 3)
        .reshape(mode_count * points, 2 * points)
    )
    far_field = product(wave_rows, backward).reshape(mode_count, points, 2, points)
    intensity = jnp.sum(far_field * far_field, axis=(0, 2))
    scaling = 1.0 - amplitude.astype(jnp.float32) / jnp.sqrt(jnp.maximum(intensity, 1.0))
    residual = (
        (far_field * scaling[None, :, None, :])
        .astype(jnp.bfloat16)
        .reshape(mode_count * points, 2 * points)
    )
    back_rows = product(residual, forward).astype(jnp.bfloat16)
    back_cols = (
        back_rows.reshape(mode_count, points, 2, points)
        .transpose(2, 1, 0, 3)
        .reshape(2 * points, mode_count * points)
    )
    update = (
        product(backward, back_cols).reshape(2, points, mode_count, points).transpose(2, 0, 1, 3)
    )
    update_real = update[:, 0]
    update_imag = update[:, 1]
    object_term = jnp.stack(
        [
            jnp.sum(probe_real * update_real + probe_imag * update_imag, 0),
            jnp.sum(probe_real * update_imag - probe_imag * update_real, 0),
        ],
        0,
    )
    probe_term = jnp.stack(
        [
            object_real * update_real + object_imag * update_imag,
            object_real * update_imag - object_imag * update_real,
        ],
        1,
    )
    return (object_term, probe_term)


def place(gradient, term, top, left):
    anchor = jnp.zeros((), jnp.int32)
    current = lax.dynamic_slice(gradient, (anchor, top, left), term.shape)
    return lax.dynamic_update_slice(gradient, current + term, (anchor, top, left))


def fold(folded, width, tile):
    pieces = ((0, width, 0), (2 * width, tile, 0), (tile + 3 * width, width, tile - width))
    result = jnp.zeros((folded.shape[0], tile, tile), jnp.float32)
    for source_row, length_row, target_row in pieces:
        for source_col, length_col, target_col in pieces:
            block = folded[
                :, source_row : source_row + length_row, source_col : source_col + length_col
            ]
            result = result.at[
                :, target_row : target_row + length_row, target_col : target_col + length_col
            ].add(block)
    return result


def shards(object_field, probe, raw_counts, resample_delta, tile_row, offsets):
    points = probe.shape[-1]
    half = points // 2
    tile = object_field.shape[1]
    tile_rows = lax.axis_size("row")
    frame_total = raw_counts.shape[0] * tile_rows * lax.axis_size("col")
    forward, backward = dft_tables(points)
    amplitudes = measure(raw_counts, resample_delta)
    extended = extended_2(object_field, (("row", 1), ("col", 2)), half)
    slot_ids = jnp.arange(tile_rows, dtype=jnp.int32)
    target = tile_row[:, 0]
    picks = (target[:, None] == slot_ids[None, :]).astype(jnp.int32)
    live = jnp.sum(picks, 0)
    slot_tops = jnp.sum(picks * offsets[:, 0:1], 0)
    slot_lefts = jnp.sum(picks * offsets[:, 1:2], 0)
    requests = jnp.stack([slot_tops, slot_lefts, live], 1)
    zero_grad = jnp.zeros(extended.shape, jnp.float32)
    zero_probe = jnp.zeros(probe.shape, jnp.float32)
    anchor = jnp.zeros((), jnp.int32)
    outgoing = jnp.einsum(
        "ks,kij->sij", picks.astype(jnp.bfloat16), amplitudes, preferred_element_type=jnp.float32
    ).astype(jnp.bfloat16)
    incoming, received = (
        lax.all_to_all(outgoing, "row", split_axis=0, concat_axis=0, tiled=True),
        lax.all_to_all(requests, "row", split_axis=0, concat_axis=0, tiled=True),
    )

    def one_slot(totals, inputs):
        amplitude, request = inputs

        def compute(state):
            gradient, probe_total = state
            window = lax.dynamic_slice(
                extended, (anchor, request[0], request[1]), (2, points, points)
            )
            object_term, probe_term = frame_terms(window, probe, amplitude, forward, backward)
            gradient = place(gradient, object_term, request[0], request[1])
            return (gradient, probe_total + probe_term)

        def skip(state):
            return state

        return (lax.cond(request[2] > 0, compute, skip, totals), None)

    (gradient, probe_total), _ = lax.scan(one_slot, (zero_grad, zero_probe), (incoming, received))
    probe_grad = lax.psum(probe_total, ("row", "col")) * (1.0 / math.sqrt(frame_total))
    folded = extended_2(gradient, (("row", 1), ("col", 2)), half)
    object_grad = fold(folded, half, tile)
    return (object_grad, probe_grad)


def solution(mesh):
    placed = (
        P(None, "row", "col"),
        P(),
        P(("row", "col"), None, None),
        P(),
        P(("row", "col"), None),
        P(("row", "col"), None),
    )
    return jax.shard_map(
        shards, mesh=mesh, in_specs=placed, out_specs=(P(None, "row", "col"), P()), check_vma=False
    )
```

profile of v0, /device:TPU:0, one launch (start us, length us, event | category | flops | bytes accessed | tf_op | source)
XLA Modules:
  0.0 630.6 jit_solution(3642967625575035420)
XLA Ops:
  7.2 3.0 copy.33
  17.0 7.0 %all-to-all-start = ((s32[8,1,3]{2,1,0:T(1,128)}), s32[8,1,3]{2,1,0:T(1,128)S(1)}, u32[]{:S(2)}, u32[]{:S(2)}) async-start(s32[8,1,3]{2,1,0:T(1,128)} %copy.31), calls=%async_computation | async-start | bytes 8192 | tf_op jit(solution)/shard_map/all_to_all | solution.py:155
  27.7 4.4 collective-permute-start.2
  35.1 8.2 %all-to-all-start.1 = ((bf16[8,256,256]{2,1,0:T(8,128)(2,1)}), bf16[8,256,256]{2,1,0:T(8,128)(2,1)S(1)}, u32[]{:S(2)}, u32[]{:S(2)}) async-start(bf16[8,256,256]{2,1,0:T(8,128)(2,1)} %copy.37), calls=%async_computation.1 | async-start | bytes 2097152 | tf_op jit(solution)/shard_map/all_to_all | solution.py:154
  49.9 3.8 pad_maximum_fusion.1
  53.7 4.9 all-to-all-done.1
  62.5 200.0 %while.22 = (s32[]{:T(128)}, f32[2,768,768]{1,2,0:T(8,128)}, f32[3,2,256,256]{2,1,3,0:T(2,128)S(1)}, s32[8,3]{1,0:T(8,128)S(1)}, f32[3,2,256,256]{2,1,3,0:T(2,12...) while((s32[]{:T(128)}, f32[2,768,768]{1,2,0:T(8,128)}, ...), condition=%wide.region_9.10_spmd, body=%wide.region_3.9_spmd.sunk | while | flops 1619984384 | bytes 79823448 | solution.py:175
  64.0 47.3 %conditional.2 = ((f32[2,768,768]{1,2,0:T(8,128)}, f32[3,2,256,256]{2,1,3,0:T(2,128)S(1)})) conditional(s32[]{:T(128)} %bitcast.80, (f32[2,768,768]{1,2,0:T(8,128)}, f32[3,2,256,256]{2,1,3,0:T(2,128)S(1)}) %tuple.93, (s32[1,3]{1,0:T(1,128)S(1)}, f32[2,768,768]{1,2,0:T(8,128)}, f32[3,2,256,256]{2,1,3,0:T(2,128)S(1)}, f32[2,768,768]{1,2,0:T(8,128)}, ...), branch_computations={%region_4.4_spmd, %region_5.8_spmd} | conditional | flops 1619984384 | bytes 79823200 | solution.py:173
  91.5 7.8 %multiply_add_fusion = (f32[3,1,256,256]{2,1,3,0:T(1,128)S(1)}, f32[3,1,256,256]{2,1,3,0:T(1,128)S(1)}, f32[256,256]{0,1:T(8,128)S(1)}, f32[256,256]{0,1:T(8,128)S(1)}) fusion(f32[256,256]{0,1:T(8,128)} %copy-done.6, f32[256,256]{0,1:T(8,128)S(1)} %get-tuple-element.273, f32[3,2,256,256]{2,1,3,0:T(2,128)S(1)} %bitcast.81, ...), kind=kLoop, calls=%fused_computation.11 | loop fusion | flops 2621440 | bytes 5767168 | tf_op jit(solution)/shard_map/while/body/eval_jaxpr/cond/branch_1_fun/add | solution.py:103
  104.6 6.7 %dynamic_update_slice.3 = f32[2,768,768]{1,2,0:T(8,128)} dynamic-update-slice(f32[2,768,768]{1,2,0:T(8,128)} %get-tuple-element.196, f32[2,256,256]{1,2,0:T(8,128)} %maximum_add_fusion.1, s32[]{:T(128)} %constant.290.clone, s32[]{:T(128)S(6)} %select_n.23, s32[]{:T(128)S(6)} %select_n.24) | dynamic-update-slice | bytes 1048580 | tf_op jit(solution)/shard_map/while/body/eval_jaxpr/cond/branch_1_fun/dynamic_update_slice | solution.py:114
  112.5 47.4 %conditional.2 = ((f32[2,768,768]{1,2,0:T(8,128)}, f32[3,2,256,256]{2,1,3,0:T(2,128)S(1)})) conditional(s32[]{:T(128)} %bitcast.80, (f32[2,768,768]{1,2,0:T(8,128)}, f32[3,2,256,256]{2,1,3,0:T(2,128)S(1)}) %tuple.93, (s32[1,3]{1,0:T(1,128)S(1)}, f32[2,768,768]{1,2,0:T(8,128)}, f32[3,2,256,256]{2,1,3,0:T(2,128)S(1)}, f32[2,768,768]{1,2,0:T(8,128)}, ...), branch_computations={%region_4.4_spmd, %region_5.8_spmd} | conditional | flops 1619984384 | bytes 79823200 | solution.py:173
  140.0 7.8 %multiply_add_fusion = (f32[3,1,256,256]{2,1,3,0:T(1,128)S(1)}, f32[3,1,256,256]{2,1,3,0:T(1,128)S(1)}, f32[256,256]{0,1:T(8,128)S(1)}, f32[256,256]{0,1:T(8,128)S(1)}) fusion(f32[256,256]{0,1:T(8,128)} %copy-done.6, f32[256,256]{0,1:T(8,128)S(1)} %get-tuple-element.273, f32[3,2,256,256]{2,1,3,0:T(2,128)S(1)} %bitcast.81, ...), kind=kLoop, calls=%fused_computation.11 | loop fusion | flops 2621440 | bytes 5767168 | tf_op jit(solution)/shard_map/while/body/eval_jaxpr/cond/branch_1_fun/add | solution.py:103
  153.2 6.8 %dynamic_update_slice.3 = f32[2,768,768]{1,2,0:T(8,128)} dynamic-update-slice(f32[2,768,768]{1,2,0:T(8,128)} %get-tuple-element.196, f32[2,256,256]{1,2,0:T(8,128)} %maximum_add_fusion.1, s32[]{:T(128)} %constant.290.clone, s32[]{:T(128)S(6)} %select_n.23, s32[]{:T(128)S(6)} %select_n.24) | dynamic-update-slice | bytes 1048580 | tf_op jit(solution)/shard_map/while/body/eval_jaxpr/cond/branch_1_fun/dynamic_update_slice | solution.py:114
  162.5 47.4 %conditional.2 = ((f32[2,768,768]{1,2,0:T(8,128)}, f32[3,2,256,256]{2,1,3,0:T(2,128)S(1)})) conditional(s32[]{:T(128)} %bitcast.80, (f32[2,768,768]{1,2,0:T(8,128)}, f32[3,2,256,256]{2,1,3,0:T(2,128)S(1)}) %tuple.93, (s32[1,3]{1,0:T(1,128)S(1)}, f32[2,768,768]{1,2,0:T(8,128)}, f32[3,2,256,256]{2,1,3,0:T(2,128)S(1)}, f32[2,768,768]{1,2,0:T(8,128)}, ...), branch_computations={%region_4.4_spmd, %region_5.8_spmd} | conditional | flops 1619984384 | bytes 79823200 | solution.py:173
  190.0 7.8 %multiply_add_fusion = (f32[3,1,256,256]{2,1,3,0:T(1,128)S(1)}, f32[3,1,256,256]{2,1,3,0:T(1,128)S(1)}, f32[256,256]{0,1:T(8,128)S(1)}, f32[256,256]{0,1:T(8,128)S(1)}) fusion(f32[256,256]{0,1:T(8,128)} %copy-done.6, f32[256,256]{0,1:T(8,128)S(1)} %get-tuple-element.273, f32[3,2,256,256]{2,1,3,0:T(2,128)S(1)} %bitcast.81, ...), kind=kLoop, calls=%fused_computation.11 | loop fusion | flops 2621440 | bytes 5767168 | tf_op jit(solution)/shard_map/while/body/eval_jaxpr/cond/branch_1_fun/add | solution.py:103
  203.1 6.7 %dynamic_update_slice.3 = f32[2,768,768]{1,2,0:T(8,128)} dynamic-update-slice(f32[2,768,768]{1,2,0:T(8,128)} %get-tuple-element.196, f32[2,256,256]{1,2,0:T(8,128)} %maximum_add_fusion.1, s32[]{:T(128)} %constant.290.clone, s32[]{:T(128)S(6)} %select_n.23, s32[]{:T(128)S(6)} %select_n.24) | dynamic-update-slice | bytes 1048580 | tf_op jit(solution)/shard_map/while/body/eval_jaxpr/cond/branch_1_fun/dynamic_update_slice | solution.py:114
  213.7 47.4 %conditional.2 = ((f32[2,768,768]{1,2,0:T(8,128)}, f32[3,2,256,256]{2,1,3,0:T(2,128)S(1)})) conditional(s32[]{:T(128)} %bitcast.80, (f32[2,768,768]{1,2,0:T(8,128)}, f32[3,2,256,256]{2,1,3,0:T(2,128)S(1)}) %tuple.93, (s32[1,3]{1,0:T(1,128)S(1)}, f32[2,768,768]{1,2,0:T(8,128)}, f32[3,2,256,256]{2,1,3,0:T(2,128)S(1)}, f32[2,768,768]{1,2,0:T(8,128)}, ...), branch_computations={%region_4.4_spmd, %region_5.8_spmd} | conditional | flops 1619984384 | bytes 79823200 | solution.py:173
  241.2 7.8 %multiply_add_fusion = (f32[3,1,256,256]{2,1,3,0:T(1,128)S(1)}, f32[3,1,256,256]{2,1,3,0:T(1,128)S(1)}, f32[256,256]{0,1:T(8,128)S(1)}, f32[256,256]{0,1:T(8,128)S(1)}) fusion(f32[256,256]{0,1:T(8,128)} %copy-done.6, f32[256,256]{0,1:T(8,128)S(1)} %get-tuple-element.273, f32[3,2,256,256]{2,1,3,0:T(2,128)S(1)} %bitcast.81, ...), kind=kLoop, calls=%fused_computation.11 | loop fusion | flops 2621440 | bytes 5767168 | tf_op jit(solution)/shard_map/while/body/eval_jaxpr/cond/branch_1_fun/add | solution.py:103
  254.4 6.7 %dynamic_update_slice.3 = f32[2,768,768]{1,2,0:T(8,128)} dynamic-update-slice(f32[2,768,768]{1,2,0:T(8,128)} %get-tuple-element.196, f32[2,256,256]{1,2,0:T(8,128)} %maximum_add_fusion.1, s32[]{:T(128)} %constant.290.clone, s32[]{:T(128)S(6)} %select_n.23, s32[]{:T(128)S(6)} %select_n.24) | dynamic-update-slice | bytes 1048580 | tf_op jit(solution)/shard_map/while/body/eval_jaxpr/cond/branch_1_fun/dynamic_update_slice | solution.py:114
  262.6 6.1 copy.41
  271.3 94.8 %collective-permute-start.4 = (f32[2,128,768]{2,1,0:T(8,128)}, f32[2,128,768]{2,1,0:T(8,128)S(1)}, u32[]{:S(2)}, u32[]{:S(2)}) collective-permute-start(f32[2,128,768]{2,1,0:T(8,128)} %get-tuple-element.287), channel_id=1, source_target_pairs={{0,4},{4,8},{8,12},{12,16},{16,20},{20,24},{24,28},{1,5},{5,9},{9,... | collective-permute-start | bytes 2359304 | tf_op jit(solution)/shard_map/ppermute | solution.py:16
  369.5 99.4 %collective-permute-done.5 = f32[2,128,768]{2,1,0:T(8,128)S(1)} collective-permute-done((f32[2,128,768]{2,1,0:T(8,128)}, f32[2,128,768]{2,1,0:T(8,128)S(1)}, u32[]{:S(2)}, u32[]{:S(2)}) %collective-permute-start.5) | collective-permute-done | bytes 786464 | tf_op jit(solution)/shard_map/ppermute | solution.py:17
  476.8 125.5 %all-reduce.3.cloned.1.call-done = f32[3,2,256,256]{3,2,1,0:T(8,128)} async-done(((f32[3,2,256,256]{3,2,1,0:T(8,128)}), f32[3,2,256,256]{3,2,1,0:T(8,128)}) %all-reduce.3.cloned.1.call-update) | async-done | bytes 1572880 | tf_op jit(solution)/shard_map/psum | solution.py:176
  610.5 3.9 scatter-add.30
  (238 shorter events, 175.0 us)
Async XLA Ops:
  7.2 16.9 %copy-start = (bf16[6,256,256]{2,1,0:T(8,128)(2,1)S(1)}, bf16[6,256,256]{2,1,0:T(8,128)(2,1)}, u32[]{:S(2)}) copy-start(bf16[6,256,256]{2,1,0:T(8,128)(2,1)} %param.32) | copy-start | bytes 2359300
  10.1 13.9 %copy-start.18 = (f32[256,256]{1,0:T(8,128)S(1)}, f32[256,256]{1,0:T(8,128)}, u32[]{:S(2)}) copy-start(f32[256,256]{1,0:T(8,128)} %param.33) | copy-start | bytes 786436
  12.4 12.5 %collective-permute-start = (f32[2,128,512]{1,2,0:T(8,128)}, f32[2,128,512]{1,2,0:T(8,128)S(1)}, u32[]{:S(2)}, u32[]{:S(2)}) collective-permute-start(f32[2,128,512]{1,2,0:T(8,128)} %get-tuple-element.291), channel_id=1, source_target_pairs={{0,4},{4,8},{8,12},{12,16},{16,20},{20,24},{24,28},{1,5},{5,9},{9,... | collective-permute-start | bytes 1572872 | tf_op jit(solution)/shard_map/ppermute | solution.py:16
  14.9 10.1 %collective-permute-start.1 = (f32[2,128,512]{1,2,0:T(8,128)}, f32[2,128,512]{1,2,0:T(8,128)S(1)}, u32[]{:S(2)}, u32[]{:S(2)}) collective-permute-start(f32[2,128,512]{1,2,0:T(8,128)} %get-tuple-element.292), channel_id=1, source_target_pairs={{4,0},{8,4},{12,8},{16,12},{20,16},{24,20},{28,24},{5,1},{9,5},{13... | collective-permute-start | bytes 1572872 | tf_op jit(solution)/shard_map/ppermute | solution.py:17
  17.0 18.0 %all-to-all-start = ((s32[8,1,3]{2,1,0:T(1,128)}), s32[8,1,3]{2,1,0:T(1,128)S(1)}, u32[]{:S(2)}, u32[]{:S(2)}) async-start(s32[8,1,3]{2,1,0:T(1,128)} %copy.31), calls=%async_computation | async-start | bytes 8192 | tf_op jit(solution)/shard_map/all_to_all | solution.py:155
  27.7 22.2 %collective-permute-start.2 = (f32[2,768,128]{1,2,0:T(8,128)}, f32[2,768,128]{1,2,0:T(8,128)}, u32[]{:S(2)}, u32[]{:S(2)}) collective-permute-start(f32[2,768,128]{1,2,0:T(8,128)} %get-tuple-element.289), channel_id=1, source_target_pairs={{0,1},{1,2},{2,3},{4,5},{5,6},{6,7},{8,9},{9,10},{10,11},{12,13},{... | collective-permute-start | bytes 2359304 | tf_op jit(solution)/shard_map/ppermute | solution.py:16
  32.0 17.9 %collective-permute-start.3 = (f32[2,768,128]{1,2,0:T(8,128)}, f32[2,768,128]{1,2,0:T(8,128)}, u32[]{:S(2)}, u32[]{:S(2)}) collective-permute-start(f32[2,768,128]{1,2,0:T(8,128)} %get-tuple-element.290), channel_id=1, source_target_pairs={{1,0},{2,1},{3,2},{5,4},{6,5},{7,6},{9,8},{10,9},{11,10},{13,12},{... | collective-permute-start | bytes 2359304 | tf_op jit(solution)/shard_map/ppermute | solution.py:17
  35.1 23.6 %all-to-all-start.1 = ((bf16[8,256,256]{2,1,0:T(8,128)(2,1)}), bf16[8,256,256]{2,1,0:T(8,128)(2,1)S(1)}, u32[]{:S(2)}, u32[]{:S(2)}) async-start(bf16[8,256,256]{2,1,0:T(8,128)(2,1)} %copy.37), calls=%async_computation.1 | async-start | bytes 2097152 | tf_op jit(solution)/shard_map/all_to_all | solution.py:154
  43.3 559.0 %all-reduce.3.cloned.1.call-start = ((), (), s32[]{:S(2)}) async-start(), calls=%async_computation.2 | async-start | bytes 3145728 | tf_op jit(solution)/shard_map/psum | solution.py:176
  64.0 10.0 %copy-start.2 = (f32[3,2,256,256]{2,1,3,0:T(2,128)}, f32[3,2,256,256]{2,1,3,0:T(2,128)S(1)}, u32[]{:S(2)}) copy-start(f32[3,2,256,256]{2,1,3,0:T(2,128)S(1)} %get-tuple-element.204) | copy-start | bytes 4718596 | tf_op jit(solution)/shard_map/while/body/eval_jaxpr/cond
  91.5 7.9 %copy-start.3 = (f32[3,2,256,256]{2,1,3,0:T(2,128)S(1)}, f32[3,2,256,256]{2,1,3,0:T(2,128)}, u32[]{:S(2)}) copy-start(f32[3,2,256,256]{2,1,3,0:T(2,128)} %copy-done.2) | copy-start | bytes 4718596 | tf_op jit(solution)/shard_map/while/body/eval_jaxpr/cond
  102.4 8.9 %copy-start.5 = (f32[3,2,256,256]{2,1,3,0:T(2,128)S(1)}, f32[3,2,256,256]{2,1,3,0:T(2,128)}, u32[]{:S(2)}) copy-start(f32[3,2,256,256]{2,1,3,0:T(2,128)} %copy-done.4) | copy-start | bytes 4718596 | tf_op jit(solution)/shard_map/while/body/eval_jaxpr/cond
  112.6 10.0 %copy-start.2 = (f32[3,2,256,256]{2,1,3,0:T(2,128)}, f32[3,2,256,256]{2,1,3,0:T(2,128)S(1)}, u32[]{:S(2)}) copy-start(f32[3,2,256,256]{2,1,3,0:T(2,128)S(1)} %get-tuple-element.204) | copy-start | bytes 4718596 | tf_op jit(solution)/shard_map/while/body/eval_jaxpr/cond
  150.9 9.1 %copy-start.5 = (f32[3,2,256,256]{2,1,3,0:T(2,128)S(1)}, f32[3,2,256,256]{2,1,3,0:T(2,128)}, u32[]{:S(2)}) copy-start(f32[3,2,256,256]{2,1,3,0:T(2,128)} %copy-done.4) | copy-start | bytes 4718596 | tf_op jit(solution)/shard_map/while/body/eval_jaxpr/cond
  162.5 10.0 %copy-start.2 = (f32[3,2,256,256]{2,1,3,0:T(2,128)}, f32[3,2,256,256]{2,1,3,0:T(2,128)S(1)}, u32[]{:S(2)}) copy-start(f32[3,2,256,256]{2,1,3,0:T(2,128)S(1)} %get-tuple-element.204) | copy-start | bytes 4718596 | tf_op jit(solution)/shard_map/while/body/eval_jaxpr/cond
  200.9 9.0 %copy-start.5 = (f32[3,2,256,256]{2,1,3,0:T(2,128)S(1)}, f32[3,2,256,256]{2,1,3,0:T(2,128)}, u32[]{:S(2)}) copy-start(f32[3,2,256,256]{2,1,3,0:T(2,128)} %copy-done.4) | copy-start | bytes 4718596 | tf_op jit(solution)/shard_map/while/body/eval_jaxpr/cond
  213.7 10.0 %copy-start.2 = (f32[3,2,256,256]{2,1,3,0:T(2,128)}, f32[3,2,256,256]{2,1,3,0:T(2,128)S(1)}, u32[]{:S(2)}) copy-start(f32[3,2,256,256]{2,1,3,0:T(2,128)S(1)} %get-tuple-element.204) | copy-start | bytes 4718596 | tf_op jit(solution)/shard_map/while/body/eval_jaxpr/cond
  241.2 7.9 %copy-start.3 = (f32[3,2,256,256]{2,1,3,0:T(2,128)S(1)}, f32[3,2,256,256]{2,1,3,0:T(2,128)}, u32[]{:S(2)}) copy-start(f32[3,2,256,256]{2,1,3,0:T(2,128)} %copy-done.2) | copy-start | bytes 4718596 | tf_op jit(solution)/shard_map/while/body/eval_jaxpr/cond
  252.1 9.0 %copy-start.5 = (f32[3,2,256,256]{2,1,3,0:T(2,128)S(1)}, f32[3,2,256,256]{2,1,3,0:T(2,128)}, u32[]{:S(2)}) copy-start(f32[3,2,256,256]{2,1,3,0:T(2,128)} %copy-done.4) | copy-start | bytes 4718596 | tf_op jit(solution)/shard_map/while/body/eval_jaxpr/cond
  271.3 98.2 %collective-permute-start.4 = (f32[2,128,768]{2,1,0:T(8,128)}, f32[2,128,768]{2,1,0:T(8,128)S(1)}, u32[]{:S(2)}, u32[]{:S(2)}) collective-permute-start(f32[2,128,768]{2,1,0:T(8,128)} %get-tuple-element.287), channel_id=1, source_target_pairs={{0,4},{4,8},{8,12},{12,16},{16,20},{20,24},{24,28},{1,5},{5,9},{9,... | collective-permute-start | bytes 2359304 | tf_op jit(solution)/shard_map/ppermute | solution.py:16
  366.1 102.8 %collective-permute-start.5 = (f32[2,128,768]{2,1,0:T(8,128)}, f32[2,128,768]{2,1,0:T(8,128)S(1)}, u32[]{:S(2)}, u32[]{:S(2)}) collective-permute-start(f32[2,128,768]{2,1,0:T(8,128)} %get-tuple-element.288), channel_id=1, source_target_pairs={{4,0},{8,4},{12,8},{16,12},{20,16},{24,20},{28,24},{5,1},{9,5},{13... | collective-permute-start | bytes 2359304 | tf_op jit(solution)/shard_map/ppermute | solution.py:17
  369.5 106.5 %copy-start.17 = (s32[3]{0:T(128)S(1)}, s32[3]{0:T(128)}, u32[]{:S(2)}) copy-start(s32[3]{0:T(128)} %constant.306.clone.1) | copy-start | bytes 40
  471.8 133.2 %collective-permute-start.6 = (f32[2,1024,128]{2,1,0:T(8,128)}, f32[2,1024,128]{2,1,0:T(8,128)}, u32[]{:S(2)}, u32[]{:S(2)}) collective-permute-start(f32[2,1024,128]{2,1,0:T(8,128)} %get-tuple-element.286), channel_id=1, source_target_pairs={{0,1},{1,2},{2,3},{4,5},{5,6},{6,7},{8,9},{9,10},{10,11},{12,13},{... | collective-permute-start | bytes 3145736 | tf_op jit(solution)/shard_map/ppermute | solution.py:16
  474.1 132.1 %collective-permute-start.7 = (f32[2,1024,128]{2,1,0:T(8,128)S(1)}, f32[2,1024,128]{2,1,0:T(8,128)}, u32[]{:S(2)}, u32[]{:S(2)}) collective-permute-start(f32[2,1024,128]{2,1,0:T(8,128)S(1)} %get-tuple-element.285), channel_id=1, source_target_pairs={{1,0},{2,1},{3,2},{5,4},{6,5},{7,6},{9,8},{10,9},{11,10},{13,12},{... | collective-permute-start | bytes 3145736 | tf_op jit(solution)/shard_map/ppermute | solution.py:17
  (27 other events, 69.2 us)
Sparse Core Ops, SparseCore 0:
  369.6 232.5 all-reduce.2
where the time goes:
time: 636 us; the launch traced here: 631 us
  waiting for transfers between devices  230 us (36%)
  starting transfers between devices  124 us (19%)
  local copies, waits for them, and re-layouts  118 us (19%)
  other arithmetic  95 us (15%)
  matrix products  27.3 us (4%)
  loops' own time  22.1 us (3%)
  between operations  14.3 us (2%)
    psum x1, waiting for transfers between devices, shards(): lax.psum(probe_total, ('row', 'col')) * (1.0 / math.sqrt(frame_total))  125 us
    ppermute x4, starting transfers between devices, extended_2(): before = lax.ppermute(last, axis, up)  104 us
    ppermute x4, waiting for transfers between devices, extended_2(): after = lax.ppermute(first, axis, down)  99.4 us
    add x4, other arithmetic, frame_terms(): object_real * update_real + object_imag * update_imag  31.4 us
    dynamic_update_slice x4, local copies, waits for them, and re-layouts, place(): lax.dynamic_update_slice(gradient, current + term, (anchor, top, left))  26.9 us
    dot_general x16, matrix products, product(): return jnp.dot(left, right, preferred_element_type=jnp.float32)  26 us
    another operation x8, loops' own time, one_slot(): return (lax.cond(request[2] > 0, compute, skip, totals), None)  16.3 us
    another operation x9, other arithmetic  14.1 us
  transfers between devices with their start and end apart: 11, of which 3 were waited for; matrix products, arithmetic and copies ran while one was open for 4% of the time, Pallas kernels for 0%

commit v1 on v0

v1 whole, which is shorter than its diff:
```python
import math

import jax
import jax.numpy as jnp
from jax import lax
from jax.experimental import pallas as pl
from jax.experimental.pallas import tpu as pltpu
from jax.sharding import PartitionSpec as P


def extended_2(value, sides, width):
    for axis, dim in sides:
        size, length = (lax.axis_size(axis), value.shape[dim])
        up = [(i, (i + 1) % size) for i in range(size - 1)]
        down = [(j, i) for i, j in up]
        last = lax.slice_in_dim(value, length - width, length, axis=dim)
        first = lax.slice_in_dim(value, 0, width, axis=dim)
        before = lax.ppermute(last, axis, up)
        after = lax.ppermute(first, axis, down)
        value = jnp.concatenate([before, value, after], axis=dim)
    return value


def product(left, right):
    return jnp.dot(left, right, preferred_element_type=jnp.float32)


def dft_tables(points):
    indices = jnp.arange(points, dtype=jnp.int32)
    phases = indices[:, None] * indices[None, :] % points
    angles = phases.astype(jnp.float32) * (2.0 * math.pi / points)
    norming = 1.0 / math.sqrt(points)
    cosine = jnp.cos(angles) * norming
    sine_part = -jnp.sin(angles) * norming
    forward = jnp.concatenate(
        [jnp.concatenate([cosine, -sine_part], 1), jnp.concatenate([sine_part, cosine], 1)], 0
    )
    backward = jnp.concatenate(
        [jnp.concatenate([cosine, sine_part], 1), jnp.concatenate([-sine_part, cosine], 1)], 0
    )
    return (forward.astype(jnp.bfloat16), backward.astype(jnp.bfloat16))


def measure(raw_counts, resample_delta):
    points = resample_delta.shape[0]
    resample = (jnp.eye(points, dtype=jnp.float32) + resample_delta).astype(jnp.bfloat16)
    first = jnp.einsum(
        "ij,kjl->kil", resample, raw_counts, preferred_element_type=jnp.float32
    ).astype(jnp.bfloat16)
    second = jnp.einsum("kij,lj->kil", first, resample, preferred_element_type=jnp.float32)
    return jnp.sqrt(jnp.maximum(second, 0.0)).astype(jnp.bfloat16)


def frames_kernel(
    requests,
    extended,
    probe,
    amplitudes,
    forward,
    backward,
    gradient,
    probe_total,
    window,
    far_field,
):
    mode_count, _, points, _ = probe.shape
    span_rows, span_cols = (points + 8, points + 128)
    gradient[...] = jnp.zeros_like(gradient)
    probe_total[...] = jnp.zeros_like(probe_total)

    def one_slot(slot, carry):
        @pl.when(requests[slot, 2] > 0)
        def _():
            top, left = (requests[slot, 0], requests[slot, 1])
            skip_rows, skip_cols = (lax.rem(top, 8), lax.rem(left, 128))
            rows = pl.ds(pl.multiple_of(top - skip_rows, 8), span_rows)
            cols = pl.ds(pl.multiple_of(left - skip_cols, 128), span_cols)
            for part in range(2):
                block = extended[part, rows, cols]
                block = pltpu.roll(block, lax.rem(span_cols - skip_cols, span_cols), 1)
                block = block[:, :points]
                block = pltpu.roll(block, lax.rem(span_rows - skip_rows, span_rows), 0)
                window[part] = block[:points]
            intensity = jnp.zeros((points, points), jnp.float32)
            for mode in range(mode_count):
                object_real, object_imag = (window[0], window[1])
                probe_real, probe_imag = (probe[mode, 0], probe[mode, 1])
                wave = jnp.concatenate(
                    [
                        (probe_real * object_real - probe_imag * object_imag).astype(jnp.bfloat16),
                        (probe_real * object_imag + probe_imag * object_real).astype(jnp.bfloat16),
                    ],
                    0,
                )
                half_done = product(forward[...], wave).astype(jnp.bfloat16)
                wave_rows = jnp.concatenate([half_done[:points], half_done[points:]], 1)
                field = product(wave_rows, backward[...])
                far_field[mode] = field
                squares = field * field
                intensity = intensity + squares[:, :points] + squares[:, points:]
            amplitude = amplitudes[slot].astype(jnp.float32)
            scaling = 1.0 - amplitude / jnp.sqrt(jnp.maximum(intensity, 1.0))
            scaling = jnp.concatenate([scaling, scaling], 1)
            term_real = jnp.zeros((points, points), jnp.float32)
            term_imag = jnp.zeros((points, points), jnp.float32)
            for mode in range(mode_count):
                residual = (far_field[mode] * scaling).astype(jnp.bfloat16)
                back_rows = product(residual, forward[...]).astype(jnp.bfloat16)
                back_cols = jnp.concatenate([back_rows[:, :points], back_rows[:, points:]], 0)
                update = product(backward[...], back_cols)
                update_real, update_imag = (update[:points], update[points:])
                object_real, object_imag = (window[0], window[1])
                probe_real, probe_imag = (probe[mode, 0], probe[mode, 1])
                term_real = term_real + (probe_real * update_real + probe_imag * update_imag)
                term_imag = term_imag + (probe_real * update_imag - probe_imag * update_real)
                probe_total[mode, 0] += object_real * update_real + object_imag * update_imag
                probe_total[mode, 1] += object_real * update_imag - object_imag * update_real
            for part, term in enumerate((term_real, term_imag)):
                block = jnp.concatenate([term, jnp.zeros((8, points), jnp.float32)], 0)
                block = pltpu.roll(block, skip_rows, 0)
                block = jnp.concatenate([block, jnp.zeros((span_rows, 128), jnp.float32)], 1)
                block = pltpu.roll(block, skip_cols, 1)
                gradient[part, rows, cols] += block

        return carry

    lax.fori_loop(0, requests.shape[0], one_slot, 0)


def frames(requests, extended, probe, amplitudes, forward, backward):
    points = probe.shape[-1]
    vmem = pl.BlockSpec(memory_space=pltpu.VMEM)
    return pl.pallas_call(
        frames_kernel,
        name="frames",
        out_shape=(
            jax.ShapeDtypeStruct(extended.shape, jnp.float32),
            jax.ShapeDtypeStruct(probe.shape, jnp.float32),
        ),
        in_specs=[pl.BlockSpec(memory_space=pltpu.SMEM)] + [vmem] * 5,
        out_specs=(vmem, vmem),
        scratch_shapes=[
            pltpu.VMEM((2, points, points), jnp.float32),
            pltpu.VMEM((probe.shape[0], points, 2 * points), jnp.float32),
        ],
        compiler_params=pltpu.CompilerParams(vmem_limit_bytes=48 * 1024 * 1024),
    )(requests, extended, probe, amplitudes, forward, backward)


def fold(folded, width, tile):
    pieces = ((0, width, 0), (2 * width, tile, 0), (tile + 3 * width, width, tile - width))
    result = jnp.zeros((folded.shape[0], tile, tile), jnp.float32)
    for source_row, length_row, target_row in pieces:
        for source_col, length_col, target_col in pieces:
            block = folded[
                :, source_row : source_row + length_row, source_col : source_col + length_col
            ]
            result = result.at[
                :, target_row : target_row + length_row, target_col : target_col + length_col
            ].add(block)
    return result


def shards(object_field, probe, raw_counts, resample_delta, tile_row, offsets):
    points = probe.shape[-1]
    half = points // 2
    tile = object_field.shape[1]
    tile_rows = lax.axis_size("row")
    frame_total = raw_counts.shape[0] * tile_rows * lax.axis_size("col")
    forward, backward = dft_tables(points)
    amplitudes = measure(raw_counts, resample_delta)
    extended = extended_2(object_field, (("row", 1), ("col", 2)), half)
    slot_ids = jnp.arange(tile_rows, dtype=jnp.int32)
    target = tile_row[:, 0]
    picks = (target[:, None] == slot_ids[None, :]).astype(jnp.int32)
    live = jnp.sum(picks, 0)
    slot_tops = jnp.sum(picks * offsets[:, 0:1], 0)
    slot_lefts = jnp.sum(picks * offsets[:, 1:2], 0)
    requests = jnp.stack([slot_tops, slot_lefts, live], 1)
    outgoing = jnp.einsum(
        "ks,kij->sij", picks.astype(jnp.bfloat16), amplitudes, preferred_element_type=jnp.float32
    ).astype(jnp.bfloat16)
    incoming, received = (
        lax.all_to_all(outgoing, "row", split_axis=0, concat_axis=0, tiled=True),
        lax.all_to_all(requests, "row", split_axis=0, concat_axis=0, tiled=True),
    )

    gradient, probe_total = frames(received, extended, probe, incoming, forward, backward)
    probe_grad = lax.psum(probe_total, ("row", "col")) * (1.0 / math.sqrt(frame_total))
    folded = extended_2(gradient, (("row", 1), ("col", 2)), half)
    object_grad = fold(folded, half, tile)
    return (object_grad, probe_grad)


def solution(mesh):
    placed = (
        P(None, "row", "col"),
        P(),
        P(("row", "col"), None, None),
        P(),
        P(("row", "col"), None),
        P(("row", "col"), None),
    )
    return jax.shard_map(
        shards, mesh=mesh, in_specs=placed, out_specs=(P(None, "row", "col"), P()), check_vma=False
    )
```

time: 636 us -> 262 us (0.41)
  local copies, waits for them, and re-layouts: 118 us -> 20.8 us
  waiting for transfers between devices: 230 us -> 140 us
  starting transfers between devices: 124 us -> 39.5 us
  other arithmetic: 95 us -> 20.8 us
  matrix products: 27.3 us -> 2 us
  Pallas kernels: 0 us -> 23.3 us
  loops' own time: 22.1 us -> 0 us
    ppermute x4, waiting for transfers between devices: 99.4 us -> 0.98 us  [extended_2(): after = lax.ppermute(first, axis, down)]
    ppermute x4, starting transfers between devices: 104 us -> 17 us  [extended_2(): before = lax.ppermute(last, axis, up)]
    add x12 -> x0, other arithmetic: 47.9 us -> none  [the longest x4 31.4 us: frame_terms(): object_real * update_real + object_imag * update_imag]
    dynamic_update_slice x4 -> x0, local copies, waits for them, and re-layouts: 26.9 us -> none  [place(): lax.dynamic_update_slice(gradient, current + term, (anchor, top, left))]
    dot_general x16 -> x1, matrix products: 26 us -> 0.37 us  [measure(): jnp.einsum('ij,kjl->kil', resample, raw_counts, preferred_element_type=jn...]
    reshape x16 -> x0, local copies, waits for them, and re-layouts: 25.4 us -> none  [the longest x4 9.02 us: frame_terms(): product(backward, back_cols).reshape(2, points, mode_count, points)]
    pallas_call x0 -> x1, Pallas kernels: none -> 23.3 us  [frames(): pl.pallas_call(frames_kernel, name='frames', out_shape=(jax.ShapeDtypeStr...]
    another operation x9 -> x0, loops' own time: 22.1 us -> none  [the longest x8 16.3 us: one_slot(): return (lax.cond(request[2] > 0, compute, skip, totals), None)]
  transfers between devices with their start and end apart: 11 -> 11, of which waited for: 3 -> 4; matrix products, arithmetic and copies ran while one was open for 4% -> 9% of each run, Pallas kernels for 0% -> 0%
where the time goes in v1:
time: 262 us; the launch traced here: 261 us
  waiting for transfers between devices  140 us (53%)
  starting transfers between devices  39.5 us (15%)
  Pallas kernels  23.3 us (9%)
  local copies, waits for them, and re-layouts  20.8 us (8%)
  other arithmetic  20.8 us (8%)
  between operations  14.4 us (5%)
    psum x1, waiting for transfers between devices, shards(): lax.psum(probe_total, ('row', 'col')) * (1.0 / math.sqrt(frame_total))  130 us
    pallas_call x1, Pallas kernels, frames(): pl.pallas_call(frames_kernel, name='frames', out_shape=(jax.ShapeDtypeStr...  23.3 us
    ppermute x4, starting transfers between devices, extended_2(): before = lax.ppermute(last, axis, up)  17 us
    all_to_all x1, starting transfers between devices, shards(): lax.all_to_all(outgoing, 'row', split_axis=0, concat_axis=0, tiled=True)  12.1 us
    all_to_all x1, waiting for transfers between devices, shards(): lax.all_to_all(outgoing, 'row', split_axis=0, concat_axis=0, tiled=True)  8.27 us
    unnamed x28, local copies, waits for them, and re-layouts  7.01 us
    another operation x5, other arithmetic  5.7 us
  transfers between devices with their start and end apart: 11, of which 4 were waited for; matrix products, arithmetic and copies ran while one was open for 9% of the time, Pallas kernels for 0%

profile of v1, /device:TPU:0, one launch (start us, length us, event | category | flops | bytes accessed | tf_op | source)
XLA Modules:
  0.0 260.8 jit_solution(2127038452771969006)
XLA Ops:
  9.5 5.2 %all-to-all-start = ((s32[8,1,3]{2,1,0:T(1,128)}), s32[8,1,3]{2,1,0:T(1,128)S(1)}, u32[]{:S(2)}, u32[]{:S(2)}) async-start(s32[8,1,3]{2,1,0:T(1,128)} %copy.10), calls=%async_computation | async-start | bytes 8192 | tf_op jit(solution)/shard_map/all_to_all | solution.py:185
  14.7 1.3 fusion.34
  16.0 2.4 collective-permute-start
  18.4 1.3 collective-permute-start.1
  23.4 1.4 fusion.33
  24.8 4.4 %collective-permute-start.2 = (f32[2,768,128]{2,1,0:T(8,128)}, f32[2,768,128]{2,1,0:T(8,128)}, u32[]{:S(2)}, u32[]{:S(2)}) collective-permute-start(f32[2,768,128]{2,1,0:T(8,128)} %get-tuple-element.129), channel_id=1, source_target_pairs={{0,1},{1,2},{2,3},{4,5},{5,6},{6,7},{8,9},{9,10},{10,11},{12,13},{... | collective-permute-start | bytes 2359304 | tf_op jit(solution)/shard_map/ppermute | solution.py:18
  29.2 1.3 collective-permute-start.3
  32.8 12.1 %all-to-all-start.1 = ((bf16[8,256,256]{2,1,0:T(8,128)(2,1)}), bf16[8,256,256]{2,1,0:T(8,128)(2,1)S(1)}, u32[]{:S(2)}, u32[]{:S(2)}) async-start(bf16[8,256,256]{2,1,0:T(8,128)(2,1)} %copy.30), calls=%async_computation.1 | async-start | bytes 2097152 | tf_op jit(solution)/shard_map/all_to_all | solution.py:184
  47.2 4.8 %pad_maximum_fusion.extended = f32[2,768,768]{2,1,0:T(8,128)} fusion(f32[2,768,128]{2,1,0:T(8,128)} %collective-permute-done.3, f32[2,768,512]{2,1,0:T(8,128)} %copy-done.2, f32[2,768,128]{2,1,0:T(8,128)} %collective-permute-done.2), kind=kLoop, calls=%fused_computation | loop fusion | flops 2359296 | bytes 9437184 | tf_op jit(solution)/shard_map/concatenate | solution.py:20
  52.1 8.3 %all-to-all-done.1.amplitudes = bf16[8,256,256]{2,1,0:T(8,128)(2,1)S(1)} async-done(((bf16[8,256,256]{2,1,0:T(8,128)(2,1)}), bf16[8,256,256]{2,1,0:T(8,128)(2,1)S(1)}, u32[]{:S(2)}, u32[]{:S(2)}) %all-to-all-start.1) | async-done | bytes 1048608 | tf_op jit(solution)/shard_map/all_to_all | solution.py:184
  60.3 1.4 copy-done.1
  61.7 23.3 %frames.1 = (f32[2,768,768]{2,1,0:T(8,128)}, f32[3,2,256,256]{3,2,1,0:T(8,128)}) custom-call(s32[8,3]{1,0:T(8,128)S(1)} %bitcast.24, f32[2,768,768]{2,1,0:T(8,128)} %pad_maximum_fusion.extended, f32[3,2,256,256]{3,2,1,0:T(8,128)S(1)} %copy-done.1, bf16[8,256,256]{2,1,0:T(8,128)(2,1)S(1)} %all-to-all-done.1.amplitudes, ...), custom_call_target="tpu_custom_call" | custom-call | tf_op jit(solution)/shard_map/frames/pallas_call | solution.py:133
  85.0 2.4 fusion.32
  87.4 6.4 %collective-permute-start.4 = (f32[2,128,768]{2,1,0:T(8,128)}, f32[2,128,768]{2,1,0:T(8,128)S(1)}, u32[]{:S(2)}, u32[]{:S(2)}) collective-permute-start(f32[2,128,768]{2,1,0:T(8,128)} %get-tuple-element.128), channel_id=1, source_target_pairs={{0,4},{4,8},{8,12},{12,16},{16,20},{20,24},{24,28},{1,5},{5,9},{9,... | collective-permute-start | bytes 2359304 | tf_op jit(solution)/shard_map/ppermute | solution.py:18
  93.8 1.3 collective-permute-start.5
  95.9 2.9 %constant_dynamic-update-slice_fusion.4 = f32[2,1024,768]{2,1,0:T(8,128)S(1)} fusion(f32[2,1024,768]{2,1,0:T(8,128)S(1)} %constant_dynamic-update-slice_fusion.5, f32[2,768,768]{2,1,0:T(8,128)} %get-tuple-element.120), kind=kLoop, calls=%fused_computation.53 | loop fusion | bytes 9437184
  100.1 3.8 %collective-permute-start.6 = (f32[2,1024,128]{2,1,0:T(8,128)S(1)}, f32[2,1024,128]{2,1,0:T(8,128)}, u32[]{:S(2)}, u32[]{:S(2)}) collective-permute-start(f32[2,1024,128]{2,1,0:T(8,128)S(1)} %get-tuple-element.126), channel_id=1, source_target_pairs={{0,1},{1,2},{2,3},{4,5},{5,6},{6,7},{8,9},{9,10},{10,11},{12,13},{... | collective-permute-start | bytes 3145736 | tf_op jit(solution)/shard_map/ppermute | solution.py:18
  103.9 1.3 collective-permute-start.7
  106.5 130.1 %all-reduce.3.cloned.1.call-done = f32[3,2,256,256]{3,2,1,0:T(8,128)} async-done(((f32[3,2,256,256]{3,2,1,0:T(8,128)}), f32[3,2,256,256]{3,2,1,0:T(8,128)}) %all-reduce.3.cloned.1.call-update) | async-done | bytes 1572880 | tf_op jit(solution)/shard_map/psum | solution.py:189
  236.6 2.8 %broadcast_multiply_fusion = f32[3,2,256,256]{3,2,1,0:T(8,128)} fusion(f32[3,2,256,256]{3,2,1,0:T(8,128)} %all-reduce.3.cloned.1.call-done), kind=kLoop, calls=%fused_computation.13 | loop fusion | flops 393216 | bytes 3145728 | tf_op jit(solution)/shard_map/mul | solution.py:189
  240.7 2.9 %add_select_fusion.1 = f32[2,128,128]{2,1,0:T(8,128)S(1)} fusion(f32[2,1024,128]{2,1,0:T(8,128)} %collective-permute-done.7, f32[2,512,512]{2,1,0:T(8,128)S(1)} %fusion.11, s32[]{:T(128)} %bitcast.11, s32[]{:T(128)} %bitcast.12, pred[]{:T(512)} %and_reduce_fusion), kind=kLoop, calls=%fused_computation.42 | loop fusion | flops 65536 | bytes 393225 | tf_op jit(solution)/shard_map/select.11
  243.6 2.5 scatter-add.30
  247.3 2.1 slice_add_fusion
  252.7 1.3 copy-done.3
  (63 shorter events, 19.4 us)
Async XLA Ops:
  7.2 12.6 %copy-start = (bf16[6,256,256]{2,1,0:T(8,128)(2,1)S(1)}, bf16[6,256,256]{2,1,0:T(8,128)(2,1)}, u32[]{:S(2)}) copy-start(bf16[6,256,256]{2,1,0:T(8,128)(2,1)} %param.28) | copy-start | bytes 2359300
  7.2 12.6 %copy-start.9 = (f32[256,256]{1,0:T(8,128)S(1)}, f32[256,256]{1,0:T(8,128)}, u32[]{:S(2)}) copy-start(f32[256,256]{1,0:T(8,128)} %param.29) | copy-start | bytes 786436
  9.5 23.4 %all-to-all-start = ((s32[8,1,3]{2,1,0:T(1,128)}), s32[8,1,3]{2,1,0:T(1,128)S(1)}, u32[]{:S(2)}, u32[]{:S(2)}) async-start(s32[8,1,3]{2,1,0:T(1,128)} %copy.10), calls=%async_computation | async-start | bytes 8192 | tf_op jit(solution)/shard_map/all_to_all | solution.py:185
  16.0 5.1 %collective-permute-start = (f32[2,128,512]{2,1,0:T(8,128)S(1)}, f32[2,128,512]{2,1,0:T(8,128)S(1)}, u32[]{:S(2)}, u32[]{:S(2)}) collective-permute-start(f32[2,128,512]{2,1,0:T(8,128)S(1)} %get-tuple-element.132), channel_id=1, source_target_pairs={{0,4},{4,8},{8,12},{12,16},{16,20},{20,24},{24,28},{1,5},{5,9},{9,... | collective-permute-start | bytes 1572872 | tf_op jit(solution)/shard_map/ppermute | solution.py:18
  18.4 4.9 %collective-permute-start.1 = (f32[2,128,512]{2,1,0:T(8,128)S(1)}, f32[2,128,512]{2,1,0:T(8,128)S(1)}, u32[]{:S(2)}, u32[]{:S(2)}) collective-permute-start(f32[2,128,512]{2,1,0:T(8,128)S(1)} %get-tuple-element.131), channel_id=1, source_target_pairs={{4,0},{8,4},{12,8},{16,12},{20,16},{24,20},{28,24},{5,1},{9,5},{13... | collective-permute-start | bytes 1572872 | tf_op jit(solution)/shard_map/ppermute | solution.py:19
  20.6 1.6 copy-start.4
  22.3 8.1 %copy-start.10 = (s32[6,1]{0,1:T(1,128)S(1)}, s32[6,1]{0,1:T(1,128)}, u32[]{:S(2)}) copy-start(s32[6,1]{0,1:T(1,128)} %param.30) | copy-start | bytes 76
  23.4 8.3 %copy-start.2 = (f32[2,768,512]{2,1,0:T(8,128)}, f32[2,768,512]{2,1,0:T(8,128)S(1)}, u32[]{:S(2)}) copy-start(f32[2,768,512]{2,1,0:T(8,128)S(1)} %constant_dynamic-update-slice_fusion) | copy-start | bytes 9437188
  24.8 22.4 %collective-permute-start.2 = (f32[2,768,128]{2,1,0:T(8,128)}, f32[2,768,128]{2,1,0:T(8,128)}, u32[]{:S(2)}, u32[]{:S(2)}) collective-permute-start(f32[2,768,128]{2,1,0:T(8,128)} %get-tuple-element.129), channel_id=1, source_target_pairs={{0,1},{1,2},{2,3},{4,5},{5,6},{6,7},{8,9},{9,10},{10,11},{12,13},{... | collective-permute-start | bytes 2359304 | tf_op jit(solution)/shard_map/ppermute | solution.py:18
  29.2 18.1 %collective-permute-start.3 = (f32[2,768,128]{2,1,0:T(8,128)}, f32[2,768,128]{2,1,0:T(8,128)}, u32[]{:S(2)}, u32[]{:S(2)}) collective-permute-start(f32[2,768,128]{2,1,0:T(8,128)} %get-tuple-element.130), channel_id=1, source_target_pairs={{1,0},{2,1},{3,2},{5,4},{6,5},{7,6},{9,8},{10,9},{11,10},{13,12},{... | collective-permute-start | bytes 2359304 | tf_op jit(solution)/shard_map/ppermute | solution.py:19
  32.8 27.5 %all-to-all-start.1 = ((bf16[8,256,256]{2,1,0:T(8,128)(2,1)}), bf16[8,256,256]{2,1,0:T(8,128)(2,1)S(1)}, u32[]{:S(2)}, u32[]{:S(2)}) async-start(bf16[8,256,256]{2,1,0:T(8,128)(2,1)} %copy.30), calls=%async_computation.1 | async-start | bytes 2097152 | tf_op jit(solution)/shard_map/all_to_all | solution.py:184
  45.0 191.6 %all-reduce.3.cloned.1.call-start = ((), (), s32[]{:S(2)}) async-start(), calls=%async_computation.2 | async-start | bytes 3145728 | tf_op jit(solution)/shard_map/psum | solution.py:189
  60.3 1.4 copy-start.1
  87.4 8.5 %collective-permute-start.4 = (f32[2,128,768]{2,1,0:T(8,128)}, f32[2,128,768]{2,1,0:T(8,128)S(1)}, u32[]{:S(2)}, u32[]{:S(2)}) collective-permute-start(f32[2,128,768]{2,1,0:T(8,128)} %get-tuple-element.128), channel_id=1, source_target_pairs={{0,4},{4,8},{8,12},{12,16},{16,20},{20,24},{24,28},{1,5},{5,9},{9,... | collective-permute-start | bytes 2359304 | tf_op jit(solution)/shard_map/ppermute | solution.py:18
  93.8 5.0 %collective-permute-start.5 = (f32[2,128,768]{2,1,0:T(8,128)S(1)}, f32[2,128,768]{2,1,0:T(8,128)S(1)}, u32[]{:S(2)}, u32[]{:S(2)}) collective-permute-start(f32[2,128,768]{2,1,0:T(8,128)S(1)} %get-tuple-element.127), channel_id=1, source_target_pairs={{4,0},{8,4},{12,8},{16,12},{20,16},{24,20},{28,24},{5,1},{9,5},{13... | collective-permute-start | bytes 2359304 | tf_op jit(solution)/shard_map/ppermute | solution.py:19
  95.9 2.9 %copy-start.7 = (f32[2,128,768]{2,1,0:T(8,128)}, f32[2,128,768]{2,1,0:T(8,128)S(1)}, u32[]{:S(2)}) copy-start(f32[2,128,768]{2,1,0:T(8,128)S(1)} %collective-permute-done.4) | copy-start | bytes 2359300
  98.8 1.2 copy-start.5
  98.9 6.9 %copy-start.11 = (s32[3]{0:T(128)S(1)}, s32[3]{0:T(128)}, u32[]{:S(2)}) copy-start(s32[3]{0:T(128)} %constant.278.clone.1) | copy-start | bytes 40
  100.1 139.3 %collective-permute-start.6 = (f32[2,1024,128]{2,1,0:T(8,128)S(1)}, f32[2,1024,128]{2,1,0:T(8,128)}, u32[]{:S(2)}, u32[]{:S(2)}) collective-permute-start(f32[2,1024,128]{2,1,0:T(8,128)S(1)} %get-tuple-element.126), channel_id=1, source_target_pairs={{0,1},{1,2},{2,3},{4,5},{5,6},{6,7},{8,9},{9,10},{10,11},{12,13},{... | collective-permute-start | bytes 3145736 | tf_op jit(solution)/shard_map/ppermute | solution.py:18
  103.9 136.8 %collective-permute-start.7 = (f32[2,1024,128]{2,1,0:T(8,128)}, f32[2,1024,128]{2,1,0:T(8,128)}, u32[]{:S(2)}, u32[]{:S(2)}) collective-permute-start(f32[2,1024,128]{2,1,0:T(8,128)} %get-tuple-element.125), channel_id=1, source_target_pairs={{1,0},{2,1},{3,2},{5,4},{6,5},{7,6},{9,8},{10,9},{11,10},{13,12},{... | collective-permute-start | bytes 3145736 | tf_op jit(solution)/shard_map/ppermute | solution.py:19
  236.6 4.0 %copy-start.8 = (f32[2,128,768]{2,1,0:T(8,128)S(1)}, f32[2,128,768]{2,1,0:T(8,128)}, u32[]{:S(2)}) copy-start(f32[2,128,768]{2,1,0:T(8,128)} %copy-done.7) | copy-start | bytes 2359300
  249.4 2.2 copy-start.6
  252.7 1.3 copy-start.3
Sparse Core Ops, SparseCore 0:
  95.3 141.2 all-reduce.2
